TPU v7x, 32 devices: a whole 2x2x4 slice. The times are simulated.
32 devices in a mesh: grp: 4 (over y, x), mem: 8 (over z, core).
Axes of the slice: x: 2, y: 2, z: 4, core: 2. Of those that a mesh axis runs over, the one named last changes fastest.
Arguments:
- factors: bfloat16 [32, 512, 2048], P(('grp', 'mem')), may hold values from -1 to 1
- occ_energy: bfloat16 [32], P(('grp', 'mem')), may hold values from -1.5 to -0.29882812
- vir_energy: bfloat16 [512], replicated, may hold values from 0.3984375 to 3
- pair_code: int32 [4, 8, 3], P('grp'), may hold values from 0 to 2
- pair_count: int32 [4, 8], P('grp'), may hold values from 1 to 3
Outputs:
- aux_density: bfloat16 [32, 512, 2048], P(('grp', 'mem'))
- lagrangian: bfloat16 [32, 512, 2048], P(('grp', 'mem'))
Inputs may be any that keep to these rules, and one draw needn't show every extreme that they name: `pair_code`: only the first pair_count entries of a device's list are read; entries may repeat.
All inputs are finite; a program needn't handle non-finite values.
Results may differ from a plain program's by a relative error of at most 0.0056.
Values may be sent and summed in bfloat16 or wider, within the bound.
No kernel may reach another device: no remote copies, remote signals or barrier semaphores. Data moves between devices by JAX's collectives and lax.ppermute only.
A program may use at most 128 MiB of HBM per device.

v0:
```python
import jax
import jax.numpy as jnp
from jax import lax
from jax.sharding import PartitionSpec as P

OCC_DEV = 1
ROUNDS = 2


def partner(value, axis, distance):
    mask = 2**distance
    pairs = [(source, source ^ mask) for source in range(lax.axis_size(axis))]
    return lax.ppermute(value, axis, pairs)


def decode_pair(code):
    round_no = code // (OCC_DEV * OCC_DEV)
    left_orb = code // OCC_DEV % OCC_DEV
    right_orb = code % OCC_DEV
    return (round_no, left_orb, right_orb)


def add_at(target, indices, contribution):
    zero_index = jnp.zeros((), jnp.int32)
    anchor = tuple(indices) + (zero_index,) * contribution.ndim
    extent = (1,) * len(indices) + contribution.shape
    current = lax.dynamic_slice(target, anchor, extent)
    return lax.dynamic_update_slice(target, current + contribution.reshape(extent), anchor)


def outer_terms(amp_tile):
    return lax.dot_general(
        amp_tile, amp_tile, (((1,), (1,)), ((), ())), preferred_element_type=jnp.float32
    )


def near_product(amp_tile, right_block):
    return jnp.dot(amp_tile, right_block, preferred_element_type=jnp.float32)


def far_product(amp_tile, left_block):
    return lax.dot_general(
        amp_tile, left_block, (((0,), (0,)), ((), ())), preferred_element_type=jnp.float32
    )


def per_device(factors, occ_energy, vir_energy, pair_code, pair_count):
    virtual = vir_energy.astype(jnp.float32)
    my_place = lax.axis_index("mem")
    group_codes = pair_code[0]
    group_counts = pair_count[0]
    my_codes = lax.dynamic_index_in_dim(group_codes, my_place, 0, keepdims=False)
    live_count = lax.dynamic_index_in_dim(group_counts, my_place, 0, keepdims=False)
    blocks_all = [factors]
    energy_list = [occ_energy]
    for round_idx in range(ROUNDS):
        visitor, visitor_energy = partner((factors, occ_energy), "mem", round_idx)
        blocks_all.append(visitor)
        energy_list.append(visitor_energy)
    stacked = jnp.stack(blocks_all)
    energy_all = jnp.stack(energy_list).astype(jnp.float32)
    vir_count = factors.shape[1]
    density_zero = jnp.zeros((vir_count, vir_count), jnp.float32)

    def pair_terms(slot_no):
        round_no, left_orb, right_orb = decode_pair(my_codes[slot_no])
        left_block = stacked[0, left_orb]
        right_block = stacked[round_no, right_orb]
        integrals = lax.dot_general(
            left_block, right_block, (((1,), (1,)), ((), ())), preferred_element_type=jnp.float32
        )
        denominator = (
            virtual[:, None]
            + virtual[None, :]
            - energy_all[0, left_orb]
            - energy_all[round_no, right_orb]
        )
        amp_tile = (integrals / denominator).astype(jnp.bfloat16)
        return (round_no, left_orb, right_orb, left_block, right_block, amp_tile)

    def pair_step(slot_no, carry_pair):
        density, totals = carry_pair
        round_no, left_orb, right_orb, left_block, right_block, amp_tile = pair_terms(slot_no)
        density = density + outer_terms(amp_tile)
        totals = add_at(
            totals, (jnp.zeros((), jnp.int32), left_orb), near_product(amp_tile, right_block)
        )
        totals = add_at(totals, (round_no, right_orb), far_product(amp_tile, left_block))
        return (density, totals)

    totals_zero = jnp.zeros((ROUNDS + 1,) + factors.shape, jnp.float32)
    density, totals = lax.fori_loop(0, live_count, pair_step, (density_zero, totals_zero))
    gathered = totals[0]
    for round_idx in range(ROUNDS):
        gathered = gathered + partner(totals[round_idx + 1], "mem", round_idx)
    density = lax.psum(density, "mem")
    density = lax.psum(density, "grp")
    density_scale = 1.0 / (8.0 * lax.axis_size("grp") * lax.axis_size("mem"))
    density_tile = (density * density_scale).astype(jnp.bfloat16)
    lagrangian = jnp.einsum(
        "ab,kbp->kap", density_tile, factors, preferred_element_type=jnp.float32
    )
    return (gathered.astype(jnp.bfloat16), lagrangian.astype(jnp.bfloat16))


def solution(mesh):
    in_specs = (
        P(("grp", "mem"), None, None),
        P(("grp", "mem")),
        P(),
        P("grp", None, None),
        P("grp", None),
    )
    out_specs = (P(("grp", "mem"), None, None), P(("grp", "mem"), None, None))
    return jax.shard_map(
        per_device, mesh=mesh, in_specs=in_specs, out_specs=out_specs, check_vma=False
    )
```

profile of v0, /device:TPU:0, one launch (start us, length us, event | category | flops | bytes accessed | tf_op | source)
XLA Modules:
  0.0 274.6 jit_solution(6055429350554140018)
XLA Ops:
  7.8 2.6 collective-permute-start.1
  11.9 1.2 constant_dynamic-slice_fusion.1
  13.4 43.7 %collective-permute-done.3 = bf16[1]{0:T(256)(128)(2,1)} collective-permute-done((bf16[1]{0:T(256)(128)(2,1)}, bf16[1]{0:T(256)(128)(2,1)}, u32[]{:S(2)}, u32[]{:S(2)}) %collective-permute-start.3) | collective-permute-done | bytes 34 | tf_op jit(solution)/shard_map/ppermute | solution.py:13
  57.1 1.3 maximum_convert_fusion
  58.3 5.5 %pad_maximum_fusion = bf16[3,1,512,2048]{3,2,1,0:T(8,128)(2,1)} fusion(bf16[1,1,512,2048]{3,2,1,0:T(8,128)(2,1)} %bitcast.11, bf16[1,1,512,2048]{3,2,1,0:T(8,128)(2,1)S(1)} %bitcast.93, bf16[1,1,512,2048]{3,2,1,0:T(8,128)(2,1)} %bitcast.92), kind=kLoop, calls=%fused_computation.19 | loop fusion | flops 6291456 | bytes 12582912 | tf_op jit(solution)/shard_map/stack | solution.py:60
  63.9 6.1 %broadcast_in_dim.9 = f32[3,1,512,2048]{3,2,1,0:T(8,128)} broadcast(f32[]{:T(128)} %constant.74.clone.1), dimensions={} | broadcast | bytes 12582916 | tf_op jit(solution)/shard_map/broadcast_in_dim | solution.py:91
  70.1 39.3 %while.14 = (s32[]{:T(128)}, f32[512,512]{1,0:T(8,128)S(1)}, f32[3,1,512,2048]{3,2,1,0:T(8,128)}, s32[]{:T(128)}, s32[3]{0:T(128)S(1)}, /*index=5*/bf16[3,1,512,...) while((s32[]{:T(128)}, f32[512,512]{1,0:T(8,128)S(1)}, ...), condition=%wide.region_1.2_spmd, body=%wide.region_0.1_spmd.sunk | while | flops 3493330944 | bytes 155194704 | solution.py:92
  74.0 6.0 %divide_convert_fusion.2 = bf16[512,512]{0,1:T(8,128)(2,1)S(1)} fusion(bf16[3,1,512,2048]{3,2,1,0:T(8,128)(2,1)} %get-tuple-element.212, s32[]{:T(128)S(6)} %select_n.46, f32[]{:T(128)} %bitcast.89, f32[]{:T(128)} %bitcast.90, f32[512]{0:T(512)S(1)} %get-tuple-element.213), kind=kOutput, calls=%fused_computation.15.clone.1 | convolution fusion | flops 1075052544 | bytes 4723716 | tf_op jit(solution)/shard_map/while/body/dot_general | solution.py:69
  80.5 1.1 copy-done.3
  81.7 1.6 fusion.53
  83.2 1.6 fusion.54
  84.9 4.5 %copy-done.2 = f32[3,1,512,2048]{3,2,1,0:T(8,128)} copy-done((f32[3,1,512,2048]{3,2,1,0:T(8,128)}, f32[3,1,512,2048]{3,2,1,0:T(8,128)S(1)}, u32[]{:S(2)}) %copy-start.2) | copy-done | bytes 12582936 | tf_op jit(solution)/shard_map/while
  93.4 6.0 %divide_convert_fusion.2 = bf16[512,512]{0,1:T(8,128)(2,1)S(1)} fusion(bf16[3,1,512,2048]{3,2,1,0:T(8,128)(2,1)} %get-tuple-element.212, s32[]{:T(128)S(6)} %select_n.46, f32[]{:T(128)} %bitcast.89, f32[]{:T(128)} %bitcast.90, f32[512]{0:T(512)S(1)} %get-tuple-element.213), kind=kOutput, calls=%fused_computation.15.clone.1 | convolution fusion | flops 1075052544 | bytes 4723716 | tf_op jit(solution)/shard_map/while/body/dot_general | solution.py:69
  99.9 1.1 copy-done.3
  101.0 1.6 fusion.53
  102.6 1.6 fusion.54
  104.2 4.5 %copy-done.2 = f32[3,1,512,2048]{3,2,1,0:T(8,128)} copy-done((f32[3,1,512,2048]{3,2,1,0:T(8,128)}, f32[3,1,512,2048]{3,2,1,0:T(8,128)S(1)}, u32[]{:S(2)}) %copy-start.2) | copy-done | bytes 12582936 | tf_op jit(solution)/shard_map/while
  109.4 8.2 %slice_bitcast_fusion.1 = (f32[1,512,2048]{2,1,0:T(8,128)}, f32[1,512,2048]{2,1,0:T(8,128)}) fusion(f32[3,1,512,2048]{3,2,1,0:T(8,128)} %get-tuple-element.109), kind=kLoop, calls=%fused_computation.24 | loop fusion | bytes 16777216 | tf_op jit(solution)/shard_map/squeeze | solution.py:95
  117.7 19.1 %collective-permute-start.4 = (f32[1,512,2048]{2,1,0:T(8,128)}, f32[1,512,2048]{2,1,0:T(8,128)}, u32[]{:S(2)}, u32[]{:S(2)}) collective-permute-start(f32[1,512,2048]{2,1,0:T(8,128)} %get-tuple-element.129), channel_id=1, source_target_pairs={{0,1},{1,0},{2,3},{3,2},{4,5},{5,4},{6,7},{7,6},{8,9},{9,8},{10,11... | collective-permute-start | bytes 12582920 | tf_op jit(solution)/shard_map/ppermute | solution.py:13
  136.8 2.0 collective-permute-start.5
  138.8 63.4 %all-reduce.3.cloned.1.call-done = f32[512,512]{1,0:T(8,128)} async-done(((f32[512,512]{1,0:T(8,128)}), f32[512,512]{1,0:T(8,128)}) %all-reduce.3.cloned.1.call-update) | async-done | bytes 1048592 | tf_op jit(solution)/shard_map/psum | solution.py:96
  202.3 54.6 %all-reduce.5.cloned.1.call-done = f32[512,512]{1,0:T(8,128)} async-done(((f32[512,512]{1,0:T(8,128)}), f32[512,512]{1,0:T(8,128)}) %all-reduce.5.cloned.1.call-update) | async-done | bytes 1048592 | tf_op jit(solution)/shard_map/psum | solution.py:97
  256.9 3.8 %fusion.24 = bf16[1,512,2048]{2,1,0:T(8,128)(2,1)} fusion(bf16[1,512,2048]{2,1,0:T(8,128)(2,1)S(1)} %copy-done.5, f32[512,512]{1,0:T(8,128)} %all-reduce.5.cloned.1.call-done), kind=kOutput, calls=%fused_computation.26 | convolution fusion | flops 1075314688 | bytes 5242880 | tf_op jit(solution)/shard_map/ab,kbp->kap/dot_general | solution.py:100
  260.7 7.1 %fusion.23 = bf16[1,512,2048]{2,1,0:T(8,128)(2,1)} fusion(f32[1,512,2048]{2,1,0:T(8,128)} %collective-permute-done.5, f32[1,512,2048]{2,1,0:T(8,128)} %collective-permute-done.4, f32[3,1,512,2048]{3,2,1,0:T(8,128)} %get-tuple-element.109), kind=kLoop, calls=%fused_computation.22 | loop fusion | flops 3145728 | bytes 14680064 | tf_op jit(solution)/shard_map/convert_element_type | solution.py:103
  (35 shorter events, 5.5 us)
Async XLA Ops:
  7.2 6.0 %copy-start = (s32[1,8,3]{1,0,2:T(1,128)S(1)}, s32[1,8,3]{1,0,2:T(1,128)}, u32[]{:S(2)}) copy-start(s32[1,8,3]{1,0,2:T(1,128)} %param.10) | copy-start | bytes 292
  7.2 195.1 %all-reduce.3.cloned.1.call-start = ((), (), s32[]{:S(2)}) async-start(), calls=%async_computation | async-start | bytes 2097152 | tf_op jit(solution)/shard_map/psum | solution.py:96
  7.2 51.1 %collective-permute-start = (bf16[1,512,2048]{2,1,0:T(8,128)(2,1)}, bf16[1,512,2048]{2,1,0:T(8,128)(2,1)S(1)}, u32[]{:S(2)}, u32[]{:S(2)}) collective-permute-start(bf16[1,512,2048]{2,1,0:T(8,128)(2,1)} %param.7), channel_id=1, source_target_pairs={{0,1},{1,0},{2,3},{3,2},{4,5},{5,4},{6,7},{7,6},{8,9},{9,8},{10,11... | collective-permute-start | bytes 6291464 | tf_op jit(solution)/shard_map/ppermute | solution.py:13
  7.8 50.5 %collective-permute-start.1 = (bf16[1,512,2048]{2,1,0:T(8,128)(2,1)}, bf16[1,512,2048]{2,1,0:T(8,128)(2,1)}, u32[]{:S(2)}, u32[]{:S(2)}) collective-permute-start(bf16[1,512,2048]{2,1,0:T(8,128)(2,1)} %param.7), channel_id=1, source_target_pairs={{0,2},{1,3},{2,0},{3,1},{4,6},{5,7},{6,4},{7,5},{8,10},{9,11},{10,... | collective-permute-start | bytes 6291464 | tf_op jit(solution)/shard_map/ppermute | solution.py:13
  10.4 46.6 %collective-permute-start.3 = (bf16[1]{0:T(256)(128)(2,1)}, bf16[1]{0:T(256)(128)(2,1)}, u32[]{:S(2)}, u32[]{:S(2)}) collective-permute-start(bf16[1]{0:T(256)(128)(2,1)} %param.8), channel_id=1, source_target_pairs={{0,2},{1,3},{2,0},{3,1},{4,6},{5,7},{6,4},{7,5},{8,10},{9,11},{10,... | collective-permute-start | bytes 14 | tf_op jit(solution)/shard_map/ppermute | solution.py:13
  10.5 46.6 %collective-permute-start.2 = (bf16[1]{0:T(256)(128)(2,1)}, bf16[1]{0:T(256)(128)(2,1)}, u32[]{:S(2)}, u32[]{:S(2)}) collective-permute-start(bf16[1]{0:T(256)(128)(2,1)} %param.8), channel_id=1, source_target_pairs={{0,1},{1,0},{2,3},{3,2},{4,5},{5,4},{6,7},{7,6},{8,9},{9,8},{10,11... | collective-permute-start | bytes 14 | tf_op jit(solution)/shard_map/ppermute | solution.py:13
  74.0 6.5 %copy-start.1 = (f32[3,1,512,2048]{3,2,1,0:T(8,128)S(1)}, f32[3,1,512,2048]{3,2,1,0:T(8,128)}, u32[]{:S(2)}) copy-start(f32[3,1,512,2048]{3,2,1,0:T(8,128)} %get-tuple-element.198) | copy-start | bytes 37748740 | tf_op jit(solution)/shard_map/while
  74.0 7.6 %copy-start.3 = (bf16[3,1,512,2048]{3,2,1,0:T(8,128)(2,1)S(1)}, bf16[3,1,512,2048]{3,2,1,0:T(8,128)(2,1)}, u32[]{:S(2)}) copy-start(bf16[3,1,512,2048]{3,2,1,0:T(8,128)(2,1)} %get-tuple-element.212) | copy-start | bytes 18874372 | tf_op jit(solution)/shard_map/while
  84.9 4.5 %copy-start.2 = (f32[3,1,512,2048]{3,2,1,0:T(8,128)}, f32[3,1,512,2048]{3,2,1,0:T(8,128)S(1)}, u32[]{:S(2)}) copy-start(f32[3,1,512,2048]{3,2,1,0:T(8,128)S(1)} %fusion.54) | copy-start | bytes 37748740 | tf_op jit(solution)/shard_map/while
  93.4 6.5 %copy-start.1 = (f32[3,1,512,2048]{3,2,1,0:T(8,128)S(1)}, f32[3,1,512,2048]{3,2,1,0:T(8,128)}, u32[]{:S(2)}) copy-start(f32[3,1,512,2048]{3,2,1,0:T(8,128)} %get-tuple-element.198) | copy-start | bytes 37748740 | tf_op jit(solution)/shard_map/while
  93.4 7.6 %copy-start.3 = (bf16[3,1,512,2048]{3,2,1,0:T(8,128)(2,1)S(1)}, bf16[3,1,512,2048]{3,2,1,0:T(8,128)(2,1)}, u32[]{:S(2)}) copy-start(bf16[3,1,512,2048]{3,2,1,0:T(8,128)(2,1)} %get-tuple-element.212) | copy-start | bytes 18874372 | tf_op jit(solution)/shard_map/while
  104.2 4.5 %copy-start.2 = (f32[3,1,512,2048]{3,2,1,0:T(8,128)}, f32[3,1,512,2048]{3,2,1,0:T(8,128)S(1)}, u32[]{:S(2)}) copy-start(f32[3,1,512,2048]{3,2,1,0:T(8,128)S(1)} %fusion.54) | copy-start | bytes 37748740 | tf_op jit(solution)/shard_map/while
  109.4 8.3 %copy-start.4 = (f32[512,512]{1,0:T(8,128)}, f32[512,512]{1,0:T(8,128)S(1)}, u32[]{:S(2)}) copy-start(f32[512,512]{1,0:T(8,128)S(1)} %get-tuple-element.110) | copy-start | bytes 3145732
  109.4 147.5 %copy-start.5 = (bf16[1,512,2048]{2,1,0:T(8,128)(2,1)S(1)}, bf16[1,512,2048]{2,1,0:T(8,128)(2,1)}, u32[]{:S(2)}) copy-start(bf16[1,512,2048]{2,1,0:T(8,128)(2,1)} %param.7) | copy-start | bytes 6291460
  117.7 143.0 %collective-permute-start.4 = (f32[1,512,2048]{2,1,0:T(8,128)}, f32[1,512,2048]{2,1,0:T(8,128)}, u32[]{:S(2)}, u32[]{:S(2)}) collective-permute-start(f32[1,512,2048]{2,1,0:T(8,128)} %get-tuple-element.129), channel_id=1, source_target_pairs={{0,1},{1,0},{2,3},{3,2},{4,5},{5,4},{6,7},{7,6},{8,9},{9,8},{10,11... | collective-permute-start | bytes 12582920 | tf_op jit(solution)/shard_map/ppermute | solution.py:13
  136.8 123.9 %collective-permute-start.5 = (f32[1,512,2048]{2,1,0:T(8,128)}, f32[1,512,2048]{2,1,0:T(8,128)}, u32[]{:S(2)}, u32[]{:S(2)}) collective-permute-start(f32[1,512,2048]{2,1,0:T(8,128)} %get-tuple-element.130), channel_id=1, source_target_pairs={{0,2},{1,3},{2,0},{3,1},{4,6},{5,7},{6,4},{7,5},{8,10},{9,11},{10,... | collective-permute-start | bytes 12582920 | tf_op jit(solution)/shard_map/ppermute | solution.py:13
  138.8 118.1 %all-reduce.5.cloned.1.call-start = ((), (), s32[]{:S(2)}) async-start(), calls=%async_computation.1 | async-start | bytes 2097152 | tf_op jit(solution)/shard_map/psum | solution.py:97
Sparse Core Ops, SparseCore 0:
  138.9 63.3 all-reduce.2
  205.3 51.5 all-reduce.4
where the time goes:
time: 275 us
  waiting for transfers between devices  162 us (59%)
  local copies, waits for them, and re-layouts  29.9 us (11%)
  starting transfers between devices  24.5 us (9%)
  matrix products  23.1 us (8%)
  between operations  14.7 us (5%)
  other arithmetic  14.5 us (5%)
  loops' own time  6.11 us (2%)
    psum x1, waiting for transfers between devices, per_device(): density = lax.psum(density, 'mem')  63.4 us
    psum x1, waiting for transfers between devices, per_device(): density = lax.psum(density, 'grp')  54.6 us
    ppermute x6, waiting for transfers between devices, partner(): return lax.ppermute(value, axis, pairs)  43.7 us
    ppermute x6, starting transfers between devices, partner(): return lax.ppermute(value, axis, pairs)  24.4 us
    dot_general x2, matrix products, pair_terms(): lax.dot_general(left_block, right_block, (((1,), (1,)), ((), ())), prefer...  12 us
    while x12, local copies, waits for them, and re-layouts  11.3 us
    squeeze x1, local copies, waits for them, and re-layouts, per_device(): gathered = gathered + partner(totals[round_idx + 1], 'mem', round_idx)  8.24 us
    convert_element_type x1, other arithmetic, per_device(): return (gathered.astype(jnp.bfloat16), lagrangian.astype(jnp.bfloat16))  7.07 us
  transfers between devices with their start and end apart: 8, of which 3 were waited for; matrix products, arithmetic and copies ran while one was open for 3% of the time, Pallas kernels for 0%

commit v1 on v0

--- a/solution.py
+++ b/solution.py
@@ -93,7 +93,7 @@
     gathered = totals[0]
     for round_idx in range(ROUNDS):
         gathered = gathered + partner(totals[round_idx + 1], "mem", round_idx)
-    density = lax.psum(density, "mem")
+    density = jnp.sum(lax.all_gather(density, "mem"), axis=0)
     density = lax.psum(density, "grp")
     density_scale = 1.0 / (8.0 * lax.axis_size("grp") * lax.axis_size("mem"))
     density_tile = (density * density_scale).astype(jnp.bfloat16)

time: 275 us -> 347 us (1.26)
  waiting for transfers between devices: 162 us -> 228 us
  other arithmetic: 14.5 us -> 20 us
    all_gather x0 -> x1, waiting for transfers between devices: none -> 133 us  [per_device(): density = jnp.sum(lax.all_gather(density, 'mem'), axis=0)]
    psum x1 -> x0, waiting for transfers between devices: 63.4 us -> none  [per_device(): density = lax.psum(density, 'mem')]
    psum x1, waiting for transfers between devices: 54.6 us -> 30.3 us  [per_device(): density = lax.psum(density, 'grp')]
    ppermute x6, waiting for transfers between devices: 43.7 us -> 63.7 us  [partner(): return lax.ppermute(value, axis, pairs)]
    reduce_sum x0 -> x1, other arithmetic: none -> 5.46 us  [per_device(): density = jnp.sum(lax.all_gather(density, 'mem'), axis=0)]
  transfers between devices with their start and end apart: 8 -> 8, of which waited for: 3 -> 4; matrix products, arithmetic and copies ran while one was open for 3% -> 7% of each run, Pallas kernels for 0% -> 0%
where the time goes in v1:
time: 347 us
  waiting for transfers between devices  228 us (66%)
  local copies, waits for them, and re-layouts  30.5 us (9%)
  starting transfers between devices  24.7 us (7%)
  matrix products  23.2 us (7%)
  other arithmetic  20 us (6%)
  between operations  14.8 us (4%)
  loops' own time  6.11 us (2%)
    all_gather x1, waiting for transfers between devices, per_device(): density = jnp.sum(lax.all_gather(density, 'mem'), axis=0)  133 us
    ppermute x6, waiting for transfers between devices, partner(): return lax.ppermute(value, axis, pairs)  63.7 us
    psum x1, waiting for transfers between devices, per_device(): density = lax.psum(density, 'grp')  30.3 us
    ppermute x6, starting transfers between devices, partner(): return lax.ppermute(value, axis, pairs)  24.6 us
    dot_general x2, matrix products, pair_terms(): lax.dot_general(left_block, right_block, (((1,), (1,)), ((), ())), prefer...  12 us
    while x12, local copies, waits for them, and re-layouts  11.3 us
    squeeze x1, local copies, waits for them, and re-layouts, per_device(): gathered = gathered + partner(totals[round_idx + 1], 'mem', round_idx)  7.94 us
    convert_element_type x1, other arithmetic, per_device(): return (gathered.astype(jnp.bfloat16), lagrangian.astype(jnp.bfloat16))  7.1 us
  transfers between devices with their start and end apart: 8, of which 4 were waited for; matrix products, arithmetic and copies ran while one was open for 7% of the time, Pallas kernels for 0%

profile of v1, /device:TPU:0, one launch (start us, length us, event | category | flops | bytes accessed | tf_op | source)
XLA Modules:
  0.0 346.8 jit_solution(15058601513326787112)
XLA Ops:
  7.8 2.6 collective-permute-start.1
  11.9 1.2 constant_dynamic-slice_fusion.1
  13.4 43.7 %collective-permute-done.3 = bf16[1]{0:T(256)(128)(2,1)} collective-permute-done((bf16[1]{0:T(256)(128)(2,1)}, bf16[1]{0:T(256)(128)(2,1)}, u32[]{:S(2)}, u32[]{:S(2)}) %collective-permute-start.3) | collective-permute-done | bytes 34 | tf_op jit(solution)/shard_map/ppermute | solution.py:13
  57.1 1.3 maximum_convert_fusion
  58.3 5.5 %pad_maximum_fusion = bf16[3,1,512,2048]{3,2,1,0:T(8,128)(2,1)} fusion(bf16[1,1,512,2048]{3,2,1,0:T(8,128)(2,1)} %bitcast.11, bf16[1,1,512,2048]{3,2,1,0:T(8,128)(2,1)S(1)} %bitcast.95, bf16[1,1,512,2048]{3,2,1,0:T(8,128)(2,1)} %bitcast.94), kind=kLoop, calls=%fused_computation.19 | loop fusion | flops 6291456 | bytes 12582912 | tf_op jit(solution)/shard_map/stack | solution.py:60
  63.9 6.1 %broadcast_in_dim.9 = f32[3,1,512,2048]{3,2,1,0:T(8,128)} broadcast(f32[]{:T(128)} %constant.75.clone.1), dimensions={} | broadcast | bytes 12582916 | tf_op jit(solution)/shard_map/broadcast_in_dim | solution.py:91
  70.1 39.4 %while.14 = (s32[]{:T(128)}, f32[512,512]{1,0:T(8,128)S(1)}, f32[3,1,512,2048]{3,2,1,0:T(8,128)}, s32[]{:T(128)}, s32[3]{0:T(128)S(1)}, /*index=5*/bf16[3,1,512,...) while((s32[]{:T(128)}, f32[512,512]{1,0:T(8,128)S(1)}, ...), condition=%wide.region_1.2_spmd, body=%wide.region_0.1_spmd.sunk | while | flops 3493330944 | bytes 155194704 | solution.py:92
  74.0 6.0 %divide_convert_fusion.2 = bf16[512,512]{0,1:T(8,128)(2,1)S(1)} fusion(bf16[3,1,512,2048]{3,2,1,0:T(8,128)(2,1)} %get-tuple-element.212, s32[]{:T(128)S(6)} %select_n.46, f32[]{:T(128)} %bitcast.90, f32[]{:T(128)} %bitcast.91, f32[512]{0:T(512)S(1)} %get-tuple-element.213), kind=kOutput, calls=%fused_computation.15.clone.1 | convolution fusion | flops 1075052544 | bytes 4723716 | tf_op jit(solution)/shard_map/while/body/dot_general | solution.py:69
  81.7 1.6 fusion.53
  83.3 1.7 fusion.54
  84.9 4.5 %copy-done.2 = f32[3,1,512,2048]{3,2,1,0:T(8,128)} copy-done((f32[3,1,512,2048]{3,2,1,0:T(8,128)}, f32[3,1,512,2048]{3,2,1,0:T(8,128)S(1)}, u32[]{:S(2)}) %copy-start.2) | copy-done | bytes 12582936 | tf_op jit(solution)/shard_map/while
  93.4 6.0 %divide_convert_fusion.2 = bf16[512,512]{0,1:T(8,128)(2,1)S(1)} fusion(bf16[3,1,512,2048]{3,2,1,0:T(8,128)(2,1)} %get-tuple-element.212, s32[]{:T(128)S(6)} %select_n.46, f32[]{:T(128)} %bitcast.90, f32[]{:T(128)} %bitcast.91, f32[512]{0:T(512)S(1)} %get-tuple-element.213), kind=kOutput, calls=%fused_computation.15.clone.1 | convolution fusion | flops 1075052544 | bytes 4723716 | tf_op jit(solution)/shard_map/while/body/dot_general | solution.py:69
  101.1 1.6 fusion.53
  102.7 1.7 fusion.54
  104.3 4.5 %copy-done.2 = f32[3,1,512,2048]{3,2,1,0:T(8,128)} copy-done((f32[3,1,512,2048]{3,2,1,0:T(8,128)}, f32[3,1,512,2048]{3,2,1,0:T(8,128)S(1)}, u32[]{:S(2)}) %copy-start.2) | copy-done | bytes 12582936 | tf_op jit(solution)/shard_map/while
  110.6 7.9 %slice_bitcast_fusion.1 = (f32[1,512,2048]{2,1,0:T(8,128)}, f32[1,512,2048]{2,1,0:T(8,128)}) fusion(f32[3,1,512,2048]{3,2,1,0:T(8,128)} %get-tuple-element.109), kind=kLoop, calls=%fused_computation.24 | loop fusion | bytes 16777216 | tf_op jit(solution)/shard_map/squeeze | solution.py:95
  118.5 19.2 %collective-permute-start.4 = (f32[1,512,2048]{2,1,0:T(8,128)}, f32[1,512,2048]{2,1,0:T(8,128)}, u32[]{:S(2)}, u32[]{:S(2)}) collective-permute-start(f32[1,512,2048]{2,1,0:T(8,128)} %get-tuple-element.129), channel_id=1, source_target_pairs={{0,1},{1,0},{2,3},{3,2},{4,5},{5,4},{6,7},{7,6},{8,9},{9,8},{10,11... | collective-permute-start | bytes 12582920 | tf_op jit(solution)/shard_map/ppermute | solution.py:13
  137.7 2.0 collective-permute-start.5
  139.7 133.4 %all-gather.3.cloned.1.call-done = f32[4096,512]{1,0:T(8,128)} async-done(((f32[512,512]{1,0:T(8,128)}), f32[4096,512]{1,0:T(8,128)}) %all-gather.3.cloned.1.call-update) | async-done | bytes 8388624 | tf_op jit(solution)/shard_map/all_gather | solution.py:96
  273.1 5.5 %reduce_sum.9 = f32[512,512]{1,0:T(8,128)} reduce(f32[8,512,512]{2,1,0:T(8,128)} %bitcast.93, f32[]{:T(128)} %constant.75.clone.1), dimensions={0}, to_apply=%region_2.3 | reduce | flops 1835008 | bytes 9437188 | tf_op jit(solution)/shard_map/reduce_sum | solution.py:96
  278.6 20.1 %collective-permute-done.5 = f32[1,512,2048]{2,1,0:T(8,128)} collective-permute-done((f32[1,512,2048]{2,1,0:T(8,128)}, f32[1,512,2048]{2,1,0:T(8,128)}, u32[]{:S(2)}, u32[]{:S(2)}) %collective-permute-start.5) | collective-permute-done | bytes 4194336 | tf_op jit(solution)/shard_map/ppermute | solution.py:13
  298.7 7.1 %fusion.23 = bf16[1,512,2048]{2,1,0:T(8,128)(2,1)} fusion(f32[1,512,2048]{2,1,0:T(8,128)} %collective-permute-done.5, f32[1,512,2048]{2,1,0:T(8,128)} %collective-permute-done.4, f32[3,1,512,2048]{3,2,1,0:T(8,128)} %get-tuple-element.109), kind=kLoop, calls=%fused_computation.22 | loop fusion | flops 3145728 | bytes 14680064 | tf_op jit(solution)/shard_map/convert_element_type | solution.py:103
  305.8 30.3 %all-reduce.2.cloned.1.call-done = f32[512,512]{1,0:T(8,128)} async-done(((f32[512,512]{1,0:T(8,128)}), f32[512,512]{1,0:T(8,128)}) %all-reduce.2.cloned.1.call-update) | async-done | bytes 1048592 | tf_op jit(solution)/shard_map/psum | solution.py:97
  336.1 3.8 %fusion.24 = bf16[1,512,2048]{2,1,0:T(8,128)(2,1)} fusion(bf16[1,512,2048]{2,1,0:T(8,128)(2,1)S(1)} %copy-done.5, f32[512,512]{1,0:T(8,128)} %all-reduce.2.cloned.1.call-done), kind=kOutput, calls=%fused_computation.26 | convolution fusion | flops 1075314688 | bytes 5242880 | tf_op jit(solution)/shard_map/ab,kbp->kap/dot_general | solution.py:100
  (36 shorter events, 8.7 us)
Async XLA Ops:
  7.2 6.0 %copy-start = (s32[1,8,3]{1,0,2:T(1,128)S(1)}, s32[1,8,3]{1,0,2:T(1,128)}, u32[]{:S(2)}) copy-start(s32[1,8,3]{1,0,2:T(1,128)} %param.10) | copy-start | bytes 292
  7.2 265.9 %all-gather.3.cloned.1.call-start = ((), (), s32[]{:S(2)}) async-start(), calls=%async_computation.1 | async-start | bytes 9437184 | tf_op jit(solution)/shard_map/all_gather | solution.py:96
  7.2 51.1 %collective-permute-start = (bf16[1,512,2048]{2,1,0:T(8,128)(2,1)}, bf16[1,512,2048]{2,1,0:T(8,128)(2,1)S(1)}, u32[]{:S(2)}, u32[]{:S(2)}) collective-permute-start(bf16[1,512,2048]{2,1,0:T(8,128)(2,1)} %param.7), channel_id=1, source_target_pairs={{0,1},{1,0},{2,3},{3,2},{4,5},{5,4},{6,7},{7,6},{8,9},{9,8},{10,11... | collective-permute-start | bytes 6291464 | tf_op jit(solution)/shard_map/ppermute | solution.py:13
  7.8 50.5 %collective-permute-start.1 = (bf16[1,512,2048]{2,1,0:T(8,128)(2,1)}, bf16[1,512,2048]{2,1,0:T(8,128)(2,1)}, u32[]{:S(2)}, u32[]{:S(2)}) collective-permute-start(bf16[1,512,2048]{2,1,0:T(8,128)(2,1)} %param.7), channel_id=1, source_target_pairs={{0,2},{1,3},{2,0},{3,1},{4,6},{5,7},{6,4},{7,5},{8,10},{9,11},{10,... | collective-permute-start | bytes 6291464 | tf_op jit(solution)/shard_map/ppermute | solution.py:13
  10.4 46.6 %collective-permute-start.3 = (bf16[1]{0:T(256)(128)(2,1)}, bf16[1]{0:T(256)(128)(2,1)}, u32[]{:S(2)}, u32[]{:S(2)}) collective-permute-start(bf16[1]{0:T(256)(128)(2,1)} %param.8), channel_id=1, source_target_pairs={{0,2},{1,3},{2,0},{3,1},{4,6},{5,7},{6,4},{7,5},{8,10},{9,11},{10,... | collective-permute-start | bytes 14 | tf_op jit(solution)/shard_map/ppermute | solution.py:13
  10.5 46.6 %collective-permute-start.2 = (bf16[1]{0:T(256)(128)(2,1)}, bf16[1]{0:T(256)(128)(2,1)}, u32[]{:S(2)}, u32[]{:S(2)}) collective-permute-start(bf16[1]{0:T(256)(128)(2,1)} %param.8), channel_id=1, source_target_pairs={{0,1},{1,0},{2,3},{3,2},{4,5},{5,4},{6,7},{7,6},{8,9},{9,8},{10,11... | collective-permute-start | bytes 14 | tf_op jit(solution)/shard_map/ppermute | solution.py:13
  74.0 6.5 %copy-start.1 = (f32[3,1,512,2048]{3,2,1,0:T(8,128)S(1)}, f32[3,1,512,2048]{3,2,1,0:T(8,128)}, u32[]{:S(2)}) copy-start(f32[3,1,512,2048]{3,2,1,0:T(8,128)} %get-tuple-element.198) | copy-start | bytes 37748740 | tf_op jit(solution)/shard_map/while
  74.0 7.6 %copy-start.3 = (bf16[3,1,512,2048]{3,2,1,0:T(8,128)(2,1)S(1)}, bf16[3,1,512,2048]{3,2,1,0:T(8,128)(2,1)}, u32[]{:S(2)}) copy-start(bf16[3,1,512,2048]{3,2,1,0:T(8,128)(2,1)} %get-tuple-element.212) | copy-start | bytes 18874372 | tf_op jit(solution)/shard_map/while
  84.9 4.5 %copy-start.2 = (f32[3,1,512,2048]{3,2,1,0:T(8,128)}, f32[3,1,512,2048]{3,2,1,0:T(8,128)S(1)}, u32[]{:S(2)}) copy-start(f32[3,1,512,2048]{3,2,1,0:T(8,128)S(1)} %fusion.54) | copy-start | bytes 37748740 | tf_op jit(solution)/shard_map/while
  93.4 6.5 %copy-start.1 = (f32[3,1,512,2048]{3,2,1,0:T(8,128)S(1)}, f32[3,1,512,2048]{3,2,1,0:T(8,128)}, u32[]{:S(2)}) copy-start(f32[3,1,512,2048]{3,2,1,0:T(8,128)} %get-tuple-element.198) | copy-start | bytes 37748740 | tf_op jit(solution)/shard_map/while
  93.4 7.6 %copy-start.3 = (bf16[3,1,512,2048]{3,2,1,0:T(8,128)(2,1)S(1)}, bf16[3,1,512,2048]{3,2,1,0:T(8,128)(2,1)}, u32[]{:S(2)}) copy-start(bf16[3,1,512,2048]{3,2,1,0:T(8,128)(2,1)} %get-tuple-element.212) | copy-start | bytes 18874372 | tf_op jit(solution)/shard_map/while
  104.3 4.5 %copy-start.2 = (f32[3,1,512,2048]{3,2,1,0:T(8,128)}, f32[3,1,512,2048]{3,2,1,0:T(8,128)S(1)}, u32[]{:S(2)}) copy-start(f32[3,1,512,2048]{3,2,1,0:T(8,128)S(1)} %fusion.54) | copy-start | bytes 37748740 | tf_op jit(solution)/shard_map/while
  109.5 1.0 copy-start.4
  110.5 225.6 %all-reduce.2.cloned.1.call-start = ((), (), s32[]{:S(2)}) async-start(), calls=%async_computation | async-start | bytes 2097152 | tf_op jit(solution)/shard_map/psum | solution.py:97
  118.5 160.1 %collective-permute-start.4 = (f32[1,512,2048]{2,1,0:T(8,128)}, f32[1,512,2048]{2,1,0:T(8,128)}, u32[]{:S(2)}, u32[]{:S(2)}) collective-permute-start(f32[1,512,2048]{2,1,0:T(8,128)} %get-tuple-element.129), channel_id=1, source_target_pairs={{0,1},{1,0},{2,3},{3,2},{4,5},{5,4},{6,7},{7,6},{8,9},{9,8},{10,11... | collective-permute-start | bytes 12582920 | tf_op jit(solution)/shard_map/ppermute | solution.py:13
  137.7 161.0 %collective-permute-start.5 = (f32[1,512,2048]{2,1,0:T(8,128)}, f32[1,512,2048]{2,1,0:T(8,128)}, u32[]{:S(2)}, u32[]{:S(2)}) collective-permute-start(f32[1,512,2048]{2,1,0:T(8,128)} %get-tuple-element.130), channel_id=1, source_target_pairs={{0,2},{1,3},{2,0},{3,1},{4,6},{5,7},{6,4},{7,5},{8,10},{9,11},{10,... | collective-permute-start | bytes 12582920 | tf_op jit(solution)/shard_map/ppermute | solution.py:13
  278.6 57.5 %copy-start.5 = (bf16[1,512,2048]{2,1,0:T(8,128)(2,1)S(1)}, bf16[1,512,2048]{2,1,0:T(8,128)(2,1)}, u32[]{:S(2)}) copy-start(bf16[1,512,2048]{2,1,0:T(8,128)(2,1)} %param.7) | copy-start | bytes 6291460
Sparse Core Ops, SparseCore 0:
  110.6 162.4 all-gather.2
  278.7 57.3 all-reduce.1
